TPU v7x, 32 devices: a whole 2x2x4 slice. The times are simulated.
32 devices in a mesh: dp: 16 (over z, y, core), inner: 2 (over x).
Axes of the slice: x: 2, y: 2, z: 4, core: 2. Of those that a mesh axis runs over, the one named last changes fastest.
Arguments:
- inputs: bfloat16 [32, 32, 32, 256], P(('dp', 'inner')), may hold values from -24 to 24
- cotangent: bfloat16 [32, 32, 32, 256], P(('dp', 'inner')), may hold values from -24 to 24
- kernel_taps: float32 [9, 256, 256], P(None, 'dp', 'inner'), may hold values from -1 to 1
Outputs:
- new_taps: float32 [9, 256, 256], P(None, 'dp', 'inner')
All inputs are finite; a program needn't handle non-finite values.
Results may differ from a plain program's by a relative error of at most 0.0003.
Values sent between devices are 32-bit elements; how exact they have to be, the bound alone decides.
No kernel may reach another device: no remote copies, remote signals or barrier semaphores. Data moves between devices by JAX's collectives and lax.ppermute only.
A program may use at most 64 MiB of HBM per device.

v0:
```python
import math
import jax
import jax.numpy as jnp
from jax import lax
from jax.sharding import PartitionSpec as P

MAPSIDE = 32
FREQS = 544
step_share = 0.06


def matmul(left_side, right_side):
    return jnp.dot(
        left_side, right_side, precision=lax.Precision.HIGHEST, preferred_element_type=jnp.float32
    )


def gradient_terms(inputs, cotangent):
    channels = inputs.shape[3]
    flat_cotangent = cotangent.reshape(-1, channels)
    collected = []
    for tap_index in range(9):
        row_off = tap_index // 3 - 1
        col_off = tap_index % 3 - 1
        shifted = jnp.roll(inputs, (-row_off, -col_off), axis=(1, 2))
        collected.append(
            lax.dot_general(
                shifted.reshape(-1, channels),
                flat_cotangent,
                (((0,), (0,)), ((), ())),
                preferred_element_type=jnp.float32,
            )
        )
    return jnp.stack(collected)


def phase_tables(freq_index, mapside, freq_count):
    row_shift = jnp.array([-1, -1, -1, 0, 0, 0, 1, 1, 1], dtype=jnp.int32)
    col_shift = jnp.array([-1, 0, 1, -1, 0, 1, -1, 0, 1], dtype=jnp.int32)
    half_width = mapside // 2 + 1
    first_freq = freq_index // half_width
    second_freq = freq_index % half_width
    turn_count = (
        first_freq[:, None] * row_shift[None, :] + second_freq[:, None] * col_shift[None, :]
    ) % mapside
    phase_angle = turn_count.astype(jnp.float32) * (2.0 * math.pi / mapside)
    live_mask = (freq_index < freq_count).astype(jnp.float32)[:, None]
    return (jnp.cos(phase_angle) * live_mask, jnp.sin(phase_angle) * live_mask)


def inverse_tables(freq_index, mapside, freq_count):
    cos_table, sin_table = phase_tables(freq_index, mapside, freq_count)
    second_freq = freq_index % (mapside // 2 + 1)
    on_edge = (second_freq == 0) | (second_freq == mapside // 2)
    weight = jnp.where(on_edge, 1.0, 2.0).astype(jnp.float32) / (mapside * mapside)
    return (cos_table * weight[:, None], sin_table * weight[:, None])


def bjorck(real_part, imag_part):
    matrix_size = real_part.shape[0]
    identity = jnp.eye(matrix_size, dtype=jnp.float32)
    for iteration in range(2):
        products = matmul(real_part.T, jnp.concatenate([real_part, imag_part], axis=1))
        square = matmul(imag_part.T, imag_part)
        cross_part = products[:, matrix_size:]
        gram_real = products[:, :matrix_size] + square
        gram_imag = cross_part - cross_part.T
        mix_real = 1.5 * identity - 0.5 * gram_real
        mix_imag = -0.5 * gram_imag
        stacked = jnp.concatenate(
            [
                jnp.concatenate([mix_real, mix_imag], axis=1),
                jnp.concatenate([-mix_imag, mix_real], axis=1),
            ],
            axis=0,
        )
        joined = matmul(jnp.concatenate([real_part, imag_part], axis=1), stacked)
        real_part, imag_part = (joined[:, :matrix_size], joined[:, matrix_size:])
    return (real_part, imag_part)


def orthonormalize(matrices):
    return bjorck(matrices[0], matrices[1])


def body(inputs, cotangent, kernel_taps):
    channels = inputs.shape[3]
    local_terms = gradient_terms(inputs, cotangent)
    partial_sum = lax.psum_scatter(local_terms, "dp", scatter_dimension=1, tiled=True)
    gradient = lax.psum_scatter(partial_sum, "inner", scatter_dimension=2, tiled=True)
    square_sum = lax.psum(jnp.sum(gradient * gradient), ("dp", "inner"))
    step_factor = step_share * math.sqrt(channels) / (jnp.sqrt(square_sum) + 1e-06)
    updated = kernel_taps - step_factor * gradient
    wide_count = lax.axis_size("dp")
    narrow = lax.axis_size("inner")
    freq_dev = -(-FREQS // (wide_count * narrow))
    in_rows = updated.shape[1]
    out_cols = updated.shape[2]
    col_blocks = lax.all_gather(updated, "inner", axis=2, tiled=True)
    gathered = lax.all_gather(col_blocks, "dp", axis=1, tiled=True)
    linear = lax.axis_index("dp") * narrow + lax.axis_index("inner")
    owned_freq = linear * freq_dev + jnp.arange(freq_dev, dtype=jnp.int32)
    cos_table, sin_table = phase_tables(owned_freq, MAPSIDE, FREQS)
    flattened = gathered.reshape(9, channels * channels)
    real_part = matmul(cos_table, flattened).reshape(freq_dev, channels, channels)
    imag_part = -matmul(sin_table, flattened).reshape(freq_dev, channels, channels)
    real_part, imag_part = lax.map(orthonormalize, (real_part, imag_part))
    returned = lax.all_to_all(
        lax.all_to_all(
            jnp.stack([real_part, imag_part], axis=1), "dp", split_axis=2, concat_axis=0, tiled=True
        ),
        "inner",
        split_axis=3,
        concat_axis=0,
        tiled=True,
    )
    slot_count = returned.shape[0]
    slot_index = jnp.arange(slot_count, dtype=jnp.int32)
    from_narrow = slot_index // (wide_count * freq_dev)
    from_wide = slot_index // freq_dev % wide_count
    freq_index = (from_wide * narrow + from_narrow) * freq_dev + slot_index % freq_dev
    weighted_cos, weighted_sin = inverse_tables(freq_index, MAPSIDE, FREQS)
    rebuilt = matmul(weighted_cos.T, returned[:, 0].reshape(slot_count, -1)) - matmul(
        weighted_sin.T, returned[:, 1].reshape(slot_count, -1)
    )
    return (math.sqrt(channels) * rebuilt).reshape(9, in_rows, out_cols)


def solution(mesh):
    placed = (
        P(("dp", "inner"), None, None, None),
        P(("dp", "inner"), None, None, None),
        P(None, "dp", "inner"),
    )
    return jax.shard_map(
        body, mesh=mesh, in_specs=placed, out_specs=P(None, "dp", "inner"), check_vma=False
    )
```

profile of v0, /device:TPU:0, one launch (start us, length us, event | category | flops | bytes accessed | tf_op | source)
XLA Modules:
  0.0 771.6 jit_solution(15128103214838415357)
XLA Ops:
  6.5 1.3 fusion.200
  12.9 1.4 copy-done.3
  14.3 66.0 %reduce-scatter.3.cloned.1.call-done = f32[9,16,256]{2,1,0:T(8,128)} async-done(((f32[9,256,256]{2,1,0:T(8,128)}), f32[9,16,256]{2,1,0:T(8,128)}) %reduce-scatter.3.cloned.1.call-update) | async-done | bytes 147472 | tf_op jit(solution)/shard_map/reduce_scatter | solution.py:89
  80.4 11.6 %reduce-scatter.5.cloned.1.call-done = f32[9,16,128]{2,1,0:T(8,128)} async-done(((f32[9,16,256]{2,1,0:T(8,128)}), f32[9,16,128]{2,1,0:T(8,128)}) %reduce-scatter.5.cloned.1.call-update) | async-done | bytes 73744 | tf_op jit(solution)/shard_map/reduce_scatter | solution.py:90
  92.0 1.5 multiply_reduce_fusion
  93.6 39.5 %psum.7 = f32[]{:T(128)} all-reduce(f32[]{:T(128)} %multiply_reduce_fusion), channel_id=1, replica_groups=mesh['dp'=16,'inner'=2] {'dp','inner'}, use_global_device_ids=true, to_apply=%region_3.4 | all-reduce | flops 1 | bytes 8 | tf_op jit(solution)/shard_map/psum | solution.py:91
  134.7 5.4 all_gather.6
  140.1 43.1 %all-gather.2.cloned.1.call-done = f32[9,256,256]{2,1,0:T(8,128)} async-done(((f32[9,16,256]{2,1,0:T(8,128)}), f32[9,256,256]{2,1,0:T(8,128)}) %all-gather.2.cloned.1.call-update) | async-done | bytes 2359312 | tf_op jit(solution)/shard_map/all_gather | solution.py:100
  183.3 1.9 slice_bitcast_fusion.2
  185.2 8.6 %fusion.41 = f32[17,256,256]{2,0,1:T(8,128)} fusion(f32[256,256,9]{1,0,2:T(8,128)S(1)} %slice_bitcast_fusion.2, f32[17]{0:T(128)S(1)} %compare_convert_fusion.1, s32[9]{0:T(128)S(1)} %copy-done.6, s32[17]{0:T(128)S(1)} %get-tuple-element.110, s32[9]{0:T(128)S(1)} %copy-done.5, s32[17]{0:T(128)S(1)} %get-tuple-element.111), kind=kOutput, calls=%fused_computation.54 | convolution fusion | flops 121440808 | bytes 6816020 | tf_op jit(solution)/shard_map/dot_general | solution.py:13
  193.8 8.6 %fusion.33 = f32[17,256,256]{2,0,1:T(8,128)} fusion(f32[256,256,9]{1,0,2:T(8,128)S(1)} %slice_bitcast_fusion.2, f32[17]{0:T(128)S(1)} %compare_convert_fusion.1, s32[9]{0:T(128)S(1)} %copy-done.6, s32[17]{0:T(128)S(1)} %get-tuple-element.110, s32[9]{0:T(128)S(1)} %copy-done.5, s32[17]{0:T(128)S(1)} %get-tuple-element.111), kind=kOutput, calls=%fused_computation.46 | convolution fusion | flops 120326696 | bytes 6816020 | tf_op jit(solution)/shard_map/dot_general | solution.py:13
  202.4 145.4 %while.12 = (s32[]{:T(128)}, f32[17,256,256]{2,1,0:T(8,128)}, f32[17,256,256]{2,1,0:T(8,128)}, f32[17,256,256]{2,0,1:T(8,128)}, f32[17,256,256]{2,0,1:T(8,128)}, /*index=5*/s32[]{:T(128)}) while((s32[]{:T(128)}, f32[17,256,256]{2,1,0:T(8,128)}, f32[17,256,256]{2,1,0:T(8,128)}, f32[17,256,256]{2,0,1:T(8,128)}, f32[17,256,256]{2,0,1:T(8,128)}, ...), condition=%wide.region_5.6_spmd, body=%wide.region_4.5_spmd.sunk | while | flops 2821455872 | bytes 14942793 | solution.py:107
  202.4 2.6 constant_dynamic-slice_fusion.3
  210.9 2.6 constant_dynamic-slice_fusion.3
  219.5 2.6 constant_dynamic-slice_fusion.3
  228.1 2.6 constant_dynamic-slice_fusion.3
  232.2 1.1 fusion.233
  236.6 2.6 constant_dynamic-slice_fusion.3
  240.7 1.1 fusion.233
  245.2 2.6 constant_dynamic-slice_fusion.3
  253.7 2.6 constant_dynamic-slice_fusion.3
  262.3 2.6 constant_dynamic-slice_fusion.3
  266.4 1.1 fusion.233
  270.9 2.6 constant_dynamic-slice_fusion.3
  279.4 2.6 constant_dynamic-slice_fusion.3
  288.0 2.6 constant_dynamic-slice_fusion.3
  292.1 1.1 fusion.233
  296.5 2.6 constant_dynamic-slice_fusion.3
  305.1 2.6 constant_dynamic-slice_fusion.3
  313.6 2.6 constant_dynamic-slice_fusion.3
  320.3 1.1 fusion.237
  322.2 2.6 constant_dynamic-slice_fusion.3
  330.7 2.6 constant_dynamic-slice_fusion.3
  334.8 1.1 fusion.233
  339.2 2.6 constant_dynamic-slice_fusion.3
  345.9 1.1 fusion.237
  347.8 4.6 pad_maximum_fusion.3
  352.4 23.6 %copy.89 = f32[17,2,256,256]{3,1,0,2:T(2,128)S(1)} copy(f32[17,2,256,256]{3,2,0,1:T(8,128)S(1)} %pad_maximum_fusion.3) | data formatting | bytes 17825792 | tf_op jit(solution)/shard_map/stack | solution.py:110
  376.0 196.4 %all_to_all.36 = f32[17,2,256,256]{3,1,0,2:T(2,128)S(1)} all-to-all(f32[17,2,256,256]{3,1,0,2:T(2,128)S(1)} %copy.89), channel_id=1, replica_groups=mesh['dp'=16,'inner'=2] {'dp'}, dimensions={2} | all-to-all | bytes 17825792 | tf_op jit(solution)/shard_map/all_to_all | solution.py:109
  572.4 1.2 copy.90
  573.7 4.5 copy.91
  578.2 11.6 %copy.92 = f32[272,2,16,256]{0,2,1,3:T(8,128)} copy(f32[272,2,16,256]{3,2,1,0:T(8,128)} %bitcast.179) | data formatting | bytes 17825792 | tf_op jit(solution)/shard_map/all_to_all | solution.py:109
  589.8 8.4 %all-to-all-start.1 = ((f32[272,2,16,256]{0,2,1,3:T(8,128)}), f32[272,2,16,256]{0,2,1,3:T(8,128)}, u32[]{:S(2)}, u32[]{:S(2)}) async-start(f32[272,2,16,256]{0,2,1,3:T(8,128)} %copy.92), calls=%async_computation.3 | async-start | bytes 25165824 | tf_op jit(solution)/shard_map/all_to_all | solution.py:108
  598.3 138.6 %all-to-all-done.1 = f32[272,2,16,256]{0,2,1,3:T(8,128)} async-done(((f32[272,2,16,256]{0,2,1,3:T(8,128)}), f32[272,2,16,256]{0,2,1,3:T(8,128)}, u32[]{:S(2)}, u32[]{:S(2)}) %all-to-all-start.1) | async-done | bytes 8912928 | tf_op jit(solution)/shard_map/all_to_all | solution.py:108
  736.8 14.6 %copy.97 = f32[272,2,16,2,128]{4,3,2,1,0:T(2,128)} copy(f32[272,2,16,2,128]{0,2,1,4,3:T(8,128)} %bitcast.42) | data formatting | bytes 17825792 | tf_op jit(solution)/shard_map/all_to_all | solution.py:108
  751.4 4.8 copy.94
  756.9 3.7 fusion.35
  760.7 3.7 fusion.47
  (292 shorter events, 99.3 us)
Async XLA Ops:
  6.5 2.9 copy-start
  6.5 2.6 copy-start.2
  6.5 73.8 %reduce-scatter.3.cloned.1.call-start = ((), (), s32[]{:S(2)}) async-start(), calls=%async_computation.4 | async-start | bytes 2506752 | tf_op jit(solution)/shard_map/reduce_scatter | solution.py:89
  12.1 121.7 %copy-start.4 = (f32[9,16,128]{2,1,0:T(8,128)S(1)}, f32[9,16,128]{2,1,0:T(8,128)}, u32[]{:S(2)}) copy-start(f32[9,16,128]{2,1,0:T(8,128)} %param.11) | copy-start | bytes 221188
  12.8 1.4 copy-start.3
  12.9 172.3 %copy-start.5 = (s32[9]{0:T(128)S(1)}, s32[9]{0:T(128)}, u32[]{:S(2)}) copy-start(s32[9]{0:T(128)} %constant.139.clone) | copy-start | bytes 112
  12.9 172.3 %copy-start.6 = (s32[9]{0:T(128)S(1)}, s32[9]{0:T(128)}, u32[]{:S(2)}) copy-start(s32[9]{0:T(128)} %constant.140.clone) | copy-start | bytes 112
  14.3 77.8 %reduce-scatter.5.cloned.1.call-start = ((), (), s32[]{:S(2)}) async-start(), calls=%async_computation.5 | async-start | bytes 221184 | tf_op jit(solution)/shard_map/reduce_scatter | solution.py:90
  80.4 102.9 %all-gather.2.cloned.1.call-start = ((), (), s32[]{:S(2)}) async-start(), calls=%async_computation.6 | async-start | bytes 2506752 | tf_op jit(solution)/shard_map/all_gather | solution.py:100
  589.8 147.1 %all-to-all-start.1 = ((f32[272,2,16,256]{0,2,1,3:T(8,128)}), f32[272,2,16,256]{0,2,1,3:T(8,128)}, u32[]{:S(2)}, u32[]{:S(2)}) async-start(f32[272,2,16,256]{0,2,1,3:T(8,128)} %copy.92), calls=%async_computation.3 | async-start | bytes 25165824 | tf_op jit(solution)/shard_map/all_to_all | solution.py:108
  756.9 8.2 %copy-start.1 = (bf16[1,32,32,256]{3,2,1,0:T(8,128)(2,1)S(1)}, bf16[1,32,32,256]{3,2,1,0:T(8,128)(2,1)}, u32[]{:S(2)}) copy-start(bf16[1,32,32,256]{3,2,1,0:T(8,128)(2,1)} %param.10) | copy-start | bytes 1572868
Sparse Core Ops, SparseCore 0:
  14.4 65.9 reduce-scatter.2
  82.6 9.4 reduce-scatter.4
  140.2 43.0 all-gather.1
where the time goes:
time: 773 us; the launch traced here: 772 us
  waiting for transfers between devices  259 us (34%)
  blocking collectives  241 us (31%)
  local copies, waits for them, and re-layouts  132 us (17%)
  matrix products  105 us (14%)
  between operations  14.1 us (2%)
  other arithmetic  9.14 us (1%)
  starting transfers between devices  8.48 us (1%)
    all_to_all x1, blocking collectives, body(): lax.all_to_all(jnp.stack([real_part, imag_part], axis=1), 'dp', split_axi...  196 us
    all_to_all x1, waiting for transfers between devices, body(): lax.all_to_all(lax.all_to_all(jnp.stack([real_part, imag_part], axis=1),...  139 us
    dot_general x106, matrix products, matmul(): jnp.dot(left_side, right_side, precision=lax.Precision.HIGHEST, preferred...  102 us
    reduce_scatter x1, waiting for transfers between devices, body(): lax.psum_scatter(local_terms, 'dp', scatter_dimension=1, tiled=True)  66 us
    dynamic_slice x51, local copies, waits for them, and re-layouts, body(): real_part, imag_part = lax.map(orthonormalize, (real_part, imag_part))  44.9 us
    all_gather x1, waiting for transfers between devices, body(): gathered = lax.all_gather(col_blocks, 'dp', axis=1, tiled=True)  43.1 us
    psum x1, blocking collectives, body(): square_sum = lax.psum(jnp.sum(gradient * gradient), ('dp', 'inner'))  39.5 us
    another operation x1, local copies, waits for them, and re-layouts, body(): jnp.stack([real_part, imag_part], axis=1)  23.6 us
  transfers between devices with their start and end apart: 4, of which 4 were waited for; matrix products, arithmetic and copies ran while one was open for 0% of the time, Pallas kernels for 0%

commit v1 on v0

--- a/solution.py
+++ b/solution.py
@@ -105,14 +105,26 @@
     real_part = matmul(cos_table, flattened).reshape(freq_dev, channels, channels)
     imag_part = -matmul(sin_table, flattened).reshape(freq_dev, channels, channels)
     real_part, imag_part = lax.map(orthonormalize, (real_part, imag_part))
-    returned = lax.all_to_all(
+    returned = jnp.concatenate(
         lax.all_to_all(
-            jnp.stack([real_part, imag_part], axis=1), "dp", split_axis=2, concat_axis=0, tiled=True
+            jnp.stack(
+                jnp.split(
+                    lax.all_to_all(
+                        jnp.stack([real_part, imag_part], axis=1),
+                        "dp",
+                        split_axis=2,
+                        concat_axis=0,
+                        tiled=True,
+                    ),
+                    lax.axis_size("inner"),
+                    axis=3,
+                )
+            ),
+            "inner",
+            0,
+            0,
         ),
-        "inner",
-        split_axis=3,
-        concat_axis=0,
-        tiled=True,
+        axis=0,
     )
     slot_count = returned.shape[0]
     slot_index = jnp.arange(slot_count, dtype=jnp.int32)

time: 773 us -> 707 us (0.915)
  waiting for transfers between devices: 259 us -> 220 us
  local copies, waits for them, and re-layouts: 132 us -> 103 us
    all_to_all x1, waiting for transfers between devices: 139 us -> 99 us  [body(): lax.all_to_all(jnp.stack(jnp.split(lax.all_to_all(jnp.stack([real_part, i...]
    all_to_all x2 -> x0, local copies, waits for them, and re-layouts: 19.4 us -> none  [body(): lax.all_to_all(lax.all_to_all(jnp.stack([real_part, imag_part], axis=1),...]
    all_to_all x3 -> x2, local copies, waits for them, and re-layouts: 17.3 us -> 2.79 us  [body(): lax.all_to_all(jnp.stack([real_part, imag_part], axis=1), 'dp', split_axi...]
where the time goes in v1:
time: 707 us; the launch traced here: 706 us
  blocking collectives  241 us (34%)
  waiting for transfers between devices  220 us (31%)
  matrix products  105 us (15%)
  local copies, waits for them, and re-layouts  103 us (15%)
  between operations  14.1 us (2%)
  other arithmetic  13.7 us (2%)
  starting transfers between devices  7.44 us (1%)
    all_to_all x1, blocking collectives, body(): lax.all_to_all(jnp.stack([real_part, imag_part], axis=1), 'dp', split_axi...  196 us
    dot_general x106, matrix products, matmul(): jnp.dot(left_side, right_side, precision=lax.Precision.HIGHEST, preferred...  102 us
    all_to_all x1, waiting for transfers between devices, body(): lax.all_to_all(jnp.stack(jnp.split(lax.all_to_all(jnp.stack([real_part, i...  99 us
    reduce_scatter x1, waiting for transfers between devices, body(): lax.psum_scatter(local_terms, 'dp', scatter_dimension=1, tiled=True)  66 us
    dynamic_slice x51, local copies, waits for them, and re-layouts, body(): real_part, imag_part = lax.map(orthonormalize, (real_part, imag_part))  44.9 us
    all_gather x1, waiting for transfers between devices, body(): gathered = lax.all_gather(col_blocks, 'dp', axis=1, tiled=True)  43.1 us
    psum x1, blocking collectives, body(): square_sum = lax.psum(jnp.sum(gradient * gradient), ('dp', 'inner'))  39.5 us
    another operation x1, local copies, waits for them, and re-layouts, body(): jnp.stack([real_part, imag_part], axis=1)  23.6 us
  transfers between devices with their start and end apart: 4, of which 4 were waited for; matrix products, arithmetic and copies ran while one was open for 0% of the time, Pallas kernels for 0%

profile of v1, /device:TPU:0, one launch (start us, length us, event | category | flops | bytes accessed | tf_op | source)
XLA Modules:
  0.0 706.4 jit_solution(18281122261173701510)
XLA Ops:
  6.5 1.3 fusion.200
  12.9 1.4 copy-done.3
  14.4 66.0 %reduce-scatter.3.cloned.1.call-done = f32[9,16,256]{2,1,0:T(8,128)} async-done(((f32[9,256,256]{2,1,0:T(8,128)}), f32[9,16,256]{2,1,0:T(8,128)}) %reduce-scatter.3.cloned.1.call-update) | async-done | bytes 147472 | tf_op jit(solution)/shard_map/reduce_scatter | solution.py:89
  80.5 11.6 %reduce-scatter.5.cloned.1.call-done = f32[9,16,128]{2,1,0:T(8,128)} async-done(((f32[9,16,256]{2,1,0:T(8,128)}), f32[9,16,128]{2,1,0:T(8,128)}) %reduce-scatter.5.cloned.1.call-update) | async-done | bytes 73744 | tf_op jit(solution)/shard_map/reduce_scatter | solution.py:90
  92.1 1.5 multiply_reduce_fusion
  93.6 39.5 %psum.7 = f32[]{:T(128)} all-reduce(f32[]{:T(128)} %multiply_reduce_fusion), channel_id=1, replica_groups=mesh['dp'=16,'inner'=2] {'dp','inner'}, use_global_device_ids=true, to_apply=%region_3.4 | all-reduce | flops 1 | bytes 8 | tf_op jit(solution)/shard_map/psum | solution.py:91
  134.7 5.4 all_gather.6
  140.2 43.1 %all-gather.2.cloned.1.call-done = f32[9,256,256]{2,1,0:T(8,128)} async-done(((f32[9,16,256]{2,1,0:T(8,128)}), f32[9,256,256]{2,1,0:T(8,128)}) %all-gather.2.cloned.1.call-update) | async-done | bytes 2359312 | tf_op jit(solution)/shard_map/all_gather | solution.py:100
  183.3 1.9 slice_bitcast_fusion.4
  185.2 8.6 %fusion.41 = f32[17,256,256]{2,0,1:T(8,128)} fusion(f32[256,256,9]{1,0,2:T(8,128)S(1)} %slice_bitcast_fusion.4, f32[17]{0:T(128)S(1)} %compare_convert_fusion.1, s32[9]{0:T(128)S(1)} %copy-done.6, s32[17]{0:T(128)S(1)} %get-tuple-element.107, s32[9]{0:T(128)S(1)} %copy-done.5, s32[17]{0:T(128)S(1)} %get-tuple-element.108), kind=kOutput, calls=%fused_computation.57 | convolution fusion | flops 121440808 | bytes 6816020 | tf_op jit(solution)/shard_map/dot_general | solution.py:13
  193.8 8.6 %fusion.33 = f32[17,256,256]{2,0,1:T(8,128)} fusion(f32[256,256,9]{1,0,2:T(8,128)S(1)} %slice_bitcast_fusion.4, f32[17]{0:T(128)S(1)} %compare_convert_fusion.1, s32[9]{0:T(128)S(1)} %copy-done.6, s32[17]{0:T(128)S(1)} %get-tuple-element.107, s32[9]{0:T(128)S(1)} %copy-done.5, s32[17]{0:T(128)S(1)} %get-tuple-element.108), kind=kOutput, calls=%fused_computation.47 | convolution fusion | flops 120326696 | bytes 6816020 | tf_op jit(solution)/shard_map/dot_general | solution.py:13
  202.4 145.3 %while.12 = (s32[]{:T(128)}, f32[17,256,256]{2,1,0:T(8,128)}, f32[17,256,256]{2,1,0:T(8,128)}, f32[17,256,256]{2,0,1:T(8,128)}, f32[17,256,256]{2,0,1:T(8,128)}, /*index=5*/s32[]{:T(128)}) while((s32[]{:T(128)}, f32[17,256,256]{2,1,0:T(8,128)}, f32[17,256,256]{2,1,0:T(8,128)}, f32[17,256,256]{2,0,1:T(8,128)}, f32[17,256,256]{2,0,1:T(8,128)}, ...), condition=%wide.region_5.6_spmd, body=%wide.region_4.5_spmd.sunk | while | flops 2821455872 | bytes 14942793 | solution.py:107
  202.4 2.6 constant_dynamic-slice_fusion.3
  211.0 2.6 constant_dynamic-slice_fusion.3
  219.5 2.6 constant_dynamic-slice_fusion.3
  226.2 1.1 fusion.237
  228.1 2.6 constant_dynamic-slice_fusion.3
  236.6 2.6 constant_dynamic-slice_fusion.3
  240.7 1.1 fusion.233
  245.2 2.6 constant_dynamic-slice_fusion.3
  249.3 1.1 fusion.233
  253.7 2.6 constant_dynamic-slice_fusion.3
  257.8 1.1 fusion.233
  262.2 2.6 constant_dynamic-slice_fusion.3
  270.8 2.6 constant_dynamic-slice_fusion.3
  279.3 2.6 constant_dynamic-slice_fusion.3
  287.9 2.6 constant_dynamic-slice_fusion.3
  292.0 1.1 fusion.233
  296.4 2.6 constant_dynamic-slice_fusion.3
  303.1 1.1 fusion.237
  305.0 2.6 constant_dynamic-slice_fusion.3
  313.5 2.6 constant_dynamic-slice_fusion.3
  317.6 1.1 fusion.233
  322.0 2.6 constant_dynamic-slice_fusion.3
  330.6 2.6 constant_dynamic-slice_fusion.3
  339.1 2.6 constant_dynamic-slice_fusion.3
  347.7 4.6 pad_maximum_fusion.3
  352.3 23.6 %copy.68 = f32[17,2,256,256]{3,1,0,2:T(2,128)S(1)} copy(f32[17,2,256,256]{3,2,0,1:T(8,128)S(1)} %pad_maximum_fusion.3) | data formatting | bytes 17825792 | tf_op jit(solution)/shard_map/stack | solution.py:113
  375.9 196.5 %all_to_all.23 = f32[17,2,256,256]{3,1,0,2:T(2,128)S(1)} all-to-all(f32[17,2,256,256]{3,1,0,2:T(2,128)S(1)} %copy.68), channel_id=1, replica_groups=mesh['dp'=16,'inner'=2] {'dp'}, dimensions={2} | all-to-all | bytes 17825792 | tf_op jit(solution)/shard_map/all_to_all | solution.py:112
  572.3 1.2 copy.69
  573.6 1.6 copy.70
  575.1 1.3 slice_bitcast_fusion.3
  576.4 4.5 pad_maximum_fusion.4
  580.9 7.4 %all-to-all-start.1 = ((f32[2,272,2,16,128]{4,3,2,1,0:T(8,128)}), f32[2,272,2,16,128]{4,3,2,1,0:T(8,128)}, u32[]{:S(2)}, u32[]{:S(2)}) async-start(f32[2,272,2,16,128]{4,3,2,1,0:T(8,128)} %pad_maximum_fusion.4), calls=%async_computation.3 | async-start | bytes 17825792 | tf_op jit(solution)/shard_map/all_to_all | solution.py:109
  588.4 99.0 %all-to-all-done.1 = f32[2,272,2,16,128]{4,3,2,1,0:T(8,128)} async-done(((f32[2,272,2,16,128]{4,3,2,1,0:T(8,128)}), f32[2,272,2,16,128]{4,3,2,1,0:T(8,128)}, u32[]{:S(2)}, u32[]{:S(2)}) %all-to-all-start.1) | async-done | bytes 8912928 | tf_op jit(solution)/shard_map/all_to_all | solution.py:109
  687.4 4.2 fusion.199
  691.7 3.7 fusion.35
  695.4 3.7 fusion.47
  (291 shorter events, 98.4 us)
Async XLA Ops:
  6.5 2.9 copy-start
  6.5 2.6 copy-start.2
  6.5 73.8 %reduce-scatter.3.cloned.1.call-start = ((), (), s32[]{:S(2)}) async-start(), calls=%async_computation.4 | async-start | bytes 2506752 | tf_op jit(solution)/shard_map/reduce_scatter | solution.py:89
  12.1 121.7 %copy-start.4 = (f32[9,16,128]{2,1,0:T(8,128)S(1)}, f32[9,16,128]{2,1,0:T(8,128)}, u32[]{:S(2)}) copy-start(f32[9,16,128]{2,1,0:T(8,128)} %param.11) | copy-start | bytes 221188
  12.8 1.4 copy-start.3
  12.9 172.3 %copy-start.5 = (s32[9]{0:T(128)S(1)}, s32[9]{0:T(128)}, u32[]{:S(2)}) copy-start(s32[9]{0:T(128)} %constant.139.clone) | copy-start | bytes 112
  12.9 172.3 %copy-start.6 = (s32[9]{0:T(128)S(1)}, s32[9]{0:T(128)}, u32[]{:S(2)}) copy-start(s32[9]{0:T(128)} %constant.140.clone) | copy-start | bytes 112
  14.3 77.8 %reduce-scatter.5.cloned.1.call-start = ((), (), s32[]{:S(2)}) async-start(), calls=%async_computation.5 | async-start | bytes 221184 | tf_op jit(solution)/shard_map/reduce_scatter | solution.py:90
  80.4 102.9 %all-gather.2.cloned.1.call-start = ((), (), s32[]{:S(2)}) async-start(), calls=%async_computation.6 | async-start | bytes 2506752 | tf_op jit(solution)/shard_map/all_gather | solution.py:100
  580.9 106.5 %all-to-all-start.1 = ((f32[2,272,2,16,128]{4,3,2,1,0:T(8,128)}), f32[2,272,2,16,128]{4,3,2,1,0:T(8,128)}, u32[]{:S(2)}, u32[]{:S(2)}) async-start(f32[2,272,2,16,128]{4,3,2,1,0:T(8,128)} %pad_maximum_fusion.4), calls=%async_computation.3 | async-start | bytes 17825792 | tf_op jit(solution)/shard_map/all_to_all | solution.py:109
  691.7 8.2 %copy-start.1 = (bf16[1,32,32,256]{3,2,1,0:T(8,128)(2,1)S(1)}, bf16[1,32,32,256]{3,2,1,0:T(8,128)(2,1)}, u32[]{:S(2)}) copy-start(bf16[1,32,32,256]{3,2,1,0:T(8,128)(2,1)} %param.10) | copy-start | bytes 1572868
Sparse Core Ops, SparseCore 0:
  14.4 65.9 reduce-scatter.2
  82.6 9.4 reduce-scatter.4
  140.2 43.0 all-gather.1
